TPU v7x, 256 devices: a whole 4x4x8 slice. The times are simulated.
256 devices in a mesh: kx: 8 (over z), ht: 8 (over y, core), real: 4 (over x).
Axes of the slice: x: 4, y: 4, z: 8, core: 2. Of those that a mesh axis runs over, the one named last changes fastest.
Arguments:
- velocity: float32 [3, 4, 32, 512, 128], P(None, 'real', 'kx', 'ht'), may hold values from -6 to 6
- low_index: int32 [8], replicated, may hold values from 0 to 31, as said below
- neighbours: int32 [32, 8], P('kx'), may hold values from 0 to 31, as said below
- owner_map: int32 [64], replicated, may hold values from 0 to 63, each once
- mode_counts: int32 [32], P('kx'), may hold values from 16 to 64
- helmholtz: float32 [64, 512, 512], P(('kx', 'ht')), may hold values from -0.25 to 0.25
Outputs:
- velocity_next: float32 [3, 4, 32, 512, 128], P(None, 'real', 'kx', 'ht')
Inputs may be any that keep to these rules, and one draw needn't show every extreme that they name: `low_index`: distinct values. neighbours[m, j] lies within 4 modes of m, counting circularly over the 32 modes; offsets of + 4 and - 4 both occur.
All inputs are finite; a program needn't handle non-finite values.
Results may differ from a plain program's by a relative error of at most 0.0001.
Values sent between devices are 32-bit elements; how exact they have to be, the bound alone decides.
A program may use at most 64 MiB of HBM per device.

v0:
```python
import jax
import jax.numpy as jnp
from jax import lax
from jax.sharding import PartitionSpec as P

dt_step = 0.1


def extended_2(block, sides, width):
    for axis, dim in sides:
        count = lax.axis_size(axis)
        forward = [(i, i + 1) for i in range(count - 1)]
        forward.append((count - 1, 0))
        backward = [(target, source) for source, target in forward]
        low = lax.ppermute(
            lax.slice_in_dim(block, block.shape[dim] - width, None, axis=dim), axis, forward
        )
        high = lax.ppermute(lax.slice_in_dim(block, 0, width, axis=dim), axis, backward)
        block = jnp.concatenate([low, block, high], axis=dim)
    return block


def spanwise_tables(mode_count, point_count):
    column_ids = jnp.arange(2 * mode_count)
    wavenumber = (column_ids // 2).astype(jnp.float32)
    imag_part = column_ids % 2
    positions = 2.0 * jnp.pi * jnp.arange(point_count).astype(jnp.float32) / point_count
    phases = wavenumber[:, None] * positions[None, :]
    forward = jnp.where(imag_part[:, None] == 0, jnp.cos(phases), -jnp.sin(phases)) / jnp.sqrt(
        jnp.float32(mode_count)
    )
    backward = forward.T * (2.0 * mode_count / point_count)
    return (forward, backward)


def apply_inverse(block, helmholtz, kx_count, ht_count, slots_dev, rows_ht):
    components, reals_dev, band_modes = (block.shape[0], block.shape[1], block.shape[2])
    regrouped = block.reshape(
        components, reals_dev, band_modes, kx_count, ht_count, slots_dev, 2, rows_ht
    )
    regrouped = regrouped.transpose(0, 1, 3, 2, 5, 6, 4, 7)
    regrouped = regrouped.reshape(
        components, reals_dev, kx_count * band_modes, slots_dev, 2, ht_count * rows_ht
    )
    solved = jnp.einsum("syx,crmspx->crmspy", helmholtz, regrouped, precision=lax.Precision.HIGHEST)
    solved = solved.reshape(
        components, reals_dev, kx_count, band_modes, slots_dev, 2, ht_count, rows_ht
    )
    solved = solved.transpose(0, 1, 3, 2, 6, 4, 5, 7)
    return solved.reshape(block.shape)


def local(velocity, low_index, neighbours, owner_map, mode_counts, helmholtz):
    highest = lax.Precision.HIGHEST
    components, reals_dev, band_modes, rows_ht, columns = velocity.shape
    kz_modes = columns // 2
    forward, backward = spanwise_tables(kz_modes, 4 * kz_modes)
    kx_count = lax.axis_size("kx")
    ht_count = lax.axis_size("ht")
    kx_total = band_modes * kx_count
    realizations = reals_dev * lax.axis_size("real")
    owners = kx_count * ht_count
    slots_dev = kz_modes // owners
    width_out = slots_dev * 2 * rows_ht
    low_members = low_index.shape[0]
    band_start = lax.axis_index("kx") * band_modes
    global_modes = band_start + jnp.arange(band_modes, dtype=jnp.int32)
    low_select = (low_index[:, None] == global_modes[None, :]).astype(jnp.float32)
    high_mask = 1.0 - jnp.sum(low_select, axis=0)
    offsets = (neighbours - global_modes[:, None] + kx_total // 2) % kx_total - kx_total // 2
    local_partner = jnp.arange(band_modes, dtype=jnp.int32)[:, None] + band_modes + offsets
    column_mask = ((jnp.arange(columns) // 2)[None, :] < mode_counts[:, None]).astype(jnp.float32)
    inverse_map = (
        jnp.zeros((kz_modes,), jnp.int32).at[owner_map].set(jnp.arange(kz_modes, dtype=jnp.int32))
    )
    current = velocity
    physical = jnp.dot(current, forward, precision=highest)
    extended = extended_2(physical, (("kx", 2),), band_modes)
    own_low = jnp.einsum("jm,crmyz->crjyz", low_select, physical, precision=highest)
    low_fields = lax.psum(own_low, "kx")
    high_low = jnp.zeros_like(physical)
    stresses = []
    for member in range(low_members):
        partner = jnp.take(extended, local_partner[:, member], axis=2)
        low_one = low_fields[:, :, member : member + 1]
        high_low = high_low + low_one * partner[1:2] + partner * low_one[1:2]
        weighted = physical * (partner[1:2] * high_mask[None, None, :, None, None])
        stresses.append(jnp.sum(weighted, axis=(1, 2)))
    stress = jnp.stack(stresses, axis=1)
    nonlinear = jnp.dot(high_low, backward, precision=highest)
    summed = lax.psum(stress, ("kx", "real"))
    low_forcing = jnp.dot(summed / realizations, backward, precision=highest)
    forcing = nonlinear * high_mask[None, None, :, None, None]
    forcing = (
        forcing + jnp.einsum("jm,cjyk->cmyk", low_select, low_forcing, precision=highest)[:, None]
    )
    forcing = forcing * column_mask[None, None, :, None, :]
    updated = current + dt_step * forcing
    slotted = jnp.take(
        updated.reshape(components, reals_dev, band_modes, rows_ht, kz_modes, 2), owner_map, axis=4
    )
    outgoing = slotted.reshape(components, reals_dev, band_modes, rows_ht, owners, slots_dev, 2)
    outgoing = outgoing.transpose(0, 1, 2, 4, 5, 6, 3)
    flat_out = outgoing.reshape(components, reals_dev, band_modes, owners, width_out)
    applied = apply_inverse(
        lax.all_to_all(flat_out, ("kx", "ht"), split_axis=3, concat_axis=3, tiled=True),
        helmholtz,
        kx_count,
        ht_count,
        slots_dev,
        rows_ht,
    )
    returned = lax.all_to_all(applied, ("kx", "ht"), split_axis=3, concat_axis=3, tiled=True)
    restored = returned.reshape(components, reals_dev, band_modes, owners, slots_dev, 2, rows_ht)
    restored = restored.transpose(0, 1, 2, 6, 3, 4, 5).reshape(
        components, reals_dev, band_modes, rows_ht, kz_modes, 2
    )
    current = jnp.take(restored, inverse_map, axis=4).reshape(
        components, reals_dev, band_modes, rows_ht, columns
    )
    return current


def solution(mesh):
    in_specs = (
        P(None, "real", "kx", "ht", None),
        P(),
        P("kx", None),
        P(),
        P("kx"),
        P(("kx", "ht"), None, None),
    )
    out_specs = P(None, "real", "kx", "ht", None)
    return jax.shard_map(local, mesh=mesh, in_specs=in_specs, out_specs=out_specs, check_vma=False)
```

profile of v0, /device:TPU:1, one launch (start us, length us, event | category | flops | bytes accessed | tf_op | source)
XLA Modules:
  0.0 327.1 jit_solution(15920989410416831472)
XLA Ops:
  6.6 2.4 fusion.12
  9.0 2.5 collective-permute-start
  11.5 4.0 %collective-permute-start.1 = (f32[3,1,4,64,256]{4,3,2,0,1:T(8,128)S(1)}, f32[3,1,4,64,256]{4,3,2,0,1:T(8,128)}, u32[]{:S(2)}, u32[]{:S(2)}) collective-permute-start(f32[3,1,4,64,256]{4,3,2,0,1:T(8,128)S(1)} %bitcast.259), channel_id=1, source_target_pairs={{32,0},{64,32},{96,64},{128,96},{160,128},{192,160},{224,192},{0,2... | collective-permute-start | bytes 2359304 | tf_op jit(solution)/shard_map/ppermute | solution.py:18
  15.6 3.1 convolution_bitcast_fusion
  18.9 0.3 slice_reduce_fusion.7
  19.8 12.9 %collective-permute-done = f32[3,1,4,64,256]{4,3,2,0,1:T(8,128)S(1)} collective-permute-done((f32[3,1,4,64,256]{4,3,2,0,1:T(8,128)S(1)}, f32[3,1,4,64,256]{4,3,2,0,1:T(8,128)S(1)}, u32[]{:S(2)}, u32[]{:S(2)}) %collective-permute-start) | collective-permute-done | bytes 786464 | tf_op jit(solution)/shard_map/ppermute | solution.py:15
  32.7 0.9 copy-done.16
  33.6 1.8 maximum_bitcast_fusion
  35.4 1.6 gather_fusion.7
  37.0 1.5 gather_fusion.5
  38.5 1.5 gather_fusion.4
  40.0 1.5 gather_fusion.3
  41.5 1.5 gather_fusion.2
  43.0 1.5 gather_fusion.1
  44.5 1.5 gather_fusion
  46.0 1.5 gather_fusion.6
  47.5 1.4 bitcast_select_fusion.2
  48.9 1.3 bitcast_select_fusion.4
  50.8 0.6 copy-done.10
  52.1 1.4 multiply_bitcast_fusion.1
  53.7 0.5 multiply_reduce_fusion
  55.4 3.9 %stack.35 = f32[3,8,64,256]{3,1,2,0:T(8,128)} concatenate(f32[3,1,64,256]{3,1,2,0:T(1,128)S(1)} %stack.27, f32[3,1,64,256]{3,1,2,0:T(1,128)S(1)} %stack.28, f32[3,1,64,256]{3,1,2,0:T(1,128)S(1)} %stack.29, f32[3,1,64,256]{3,1,2,0:T(1,128)S(1)} %stack.30, f32[3,1,64,256]{3,1,2,0:T(1,128)S(1)} %stack.31, f32[3,1,64,256]{3,1,2,0:T(1,128)S(1)} %stack.32, ...), dimensions={1} | concatenate | bytes 3145728 | tf_op jit(solution)/shard_map/stack | solution.py:89
  59.3 0.5 copy-done.31
  59.8 0.5 compare_and_fusion.1
  60.4 35.1 %all-reduce.3.cloned.1.call-done = f32[3,1,8,64,256]{4,2,3,0,1:T(8,128)} async-done(((f32[3,1,8,64,256]{4,2,3,0,1:T(8,128)}), f32[3,1,8,64,256]{4,2,3,0,1:T(8,128)}) %all-reduce.3.cloned.1.call-update) | async-done | bytes 1572880 | tf_op jit(solution)/shard_map/psum | solution.py:80
  95.5 7.7 %fusion.51 = (f32[3,1,1,64,256]{4,2,3,0,1:T(1,128)S(1)}, f32[3,1,1,64,256]{4,2,3,0,1:T(1,128)S(1)}, f32[3,1,1,64,256]{4,2,3,0,1:T(1,128)S(1)}, f32[3,1,1,64,256]...) fusion(f32[3,1,8,64,256]{4,2,3,0,1:T(8,128)} %all-reduce.3.clon, ...), kind=kLoop, calls=%fused_computation.172 | loop fusion | bytes 3145728 | tf_op jit(solution)/shard_map/slice | solution.py:85
  103.2 0.7 copy.102
  103.8 0.7 copy.103
  104.5 0.7 copy.104
  105.2 0.7 copy.105
  105.9 0.7 copy.106
  106.6 0.7 copy.107
  107.3 0.7 copy.108
  108.0 0.7 copy.109
  108.7 3.5 %fusion.52 = (f32[1,1,1,64,256]{4,2,3,0,1:T(1,128)S(1)}, f32[1,1,1,64,256]{4,2,3,0,1:T(1,128)S(1)}, f32[1,1,1,64,256]{4,2,3,0,1:T(1,128)S(1)}, f32[1,1,1,64,256]...) fusion(f32[3,1,8,64,256]{4,2,3,0,1:T(8,128)} %all-reduce.3.clon, ...), kind=kLoop, calls=%fused_computation.173 | loop fusion | bytes 1048576 | tf_op jit(solution)/shard_map/slice | solution.py:86
  112.2 0.6 copy.112
  112.8 0.6 copy.113
  113.5 0.6 copy.114
  114.1 0.6 copy.115
  114.7 0.6 copy.116
  115.3 0.6 copy.117
  116.0 133.7 %all-reduce.5.cloned.1.call-done = f32[3,8,64,256]{3,1,2,0:T(8,128)} async-done(((f32[3,8,64,256]{3,1,2,0:T(8,128)}), f32[3,8,64,256]{3,1,2,0:T(8,128)}) %all-reduce.5.cloned.1.call-update) | async-done | bytes 1572880 | tf_op jit(solution)/shard_map/psum | solution.py:91
  249.7 3.5 %fusion = f32[3,8,64,128]{3,1,2,0:T(8,128)S(1)} fusion(f32[3,8,64,256]{3,1,2,0:T(8,128)} %all-reduce.5.cloned.1.call-done, f32[256]{0:T(256)S(1)} %convert_multiply_fusion, f32[128]{0:T(128)} %copy-done.17, pred[128]{0:T(512)(128)(4,1)S(1)} %fusion.42), kind=kOutput, calls=%fused_computation.12 | convolution fusion | flops 604504064 | bytes 2360960 | tf_op jit(solution)/shard_map/dot_general | solution.py:92
  253.2 1.2 fusion.50
  254.4 5.9 %fusion.6 = f32[3,1,4,64,128]{4,3,2,0,1:T(8,128)} fusion(f32[3,1,4,64,128]{4,3,2,1,0:T(8,128)S(1)} %copy-done.14, f32[3,64,128,4]{2,3,1,0:T(4,128)S(1)} %fusion.50, f32[4,128]{1,0:T(4,128)S(1)} %compare_convert_fusion.1, f32[4]{0:T(128)} %copy-done.27, f32[256]{0:T(256)S(1)} %convert_multiply_fusion, f32[128]{0:T(128)} %copy-done.17, ...), kind=kOutput, calls=%fused_computation.21 | convolution fusion | flops 310280192 | bytes 11669168 | tf_op jit(solution)/shard_map/dot_general | solution.py:90
  260.3 1.3 copy.38
  261.6 0.5 copy.101
  262.1 1.0 gather_fusion.8
  263.2 0.2 fusion.7
  263.4 0.4 copy.55
  263.8 0.6 reshape.457
  264.4 27.5 %all_to_all.10 = f32[3,1,4,64,128]{4,2,0,1,3:T(4,128)S(1)} all-to-all(f32[3,1,4,64,128]{4,2,0,1,3:T(4,128)S(1)} %reshape.457), channel_id=1, replica_groups=mesh['kx'=8,'ht'=8,'real'=4] {'kx','ht'}, dimensions={3} | all-to-all | bytes 786432 | tf_op jit(solution)/shard_map/all_to_all | solution.py:106
  292.0 0.5 reshape.287
  292.8 1.5 convolution_bitcast_fusion.1
  294.3 0.6 copy.56
  294.9 1.3 reshape.459
  296.2 5.5 %all-to-all-start.1 = ((f32[3,1,4,64,128]{4,2,0,1,3:T(4,128)}), f32[3,1,4,64,128]{4,2,0,1,3:T(4,128)S(1)}, u32[]{:S(2)}, u32[]{:S(2)}) async-start(f32[3,1,4,64,128]{4,2,0,1,3:T(4,128)} %reshape.459), calls=%async_computation.1 | async-start | bytes 786432 | tf_op jit(solution)/shard_map/all_to_all | solution.py:113
  301.6 0.9 scatter_custom_fusion
  302.6 14.2 %all-to-all-done.1 = f32[3,1,4,64,128]{4,2,0,1,3:T(4,128)S(1)} async-done(((f32[3,1,4,64,128]{4,2,0,1,3:T(4,128)}), f32[3,1,4,64,128]{4,2,0,1,3:T(4,128)S(1)}, u32[]{:S(2)}, u32[]{:S(2)}) %all-to-all-start.1) | async-done | bytes 393248 | tf_op jit(solution)/shard_map/all_to_all | solution.py:113
  316.8 0.5 reshape.460
  317.5 1.1 gather_fusion.9
  318.6 0.2 bitcast_select_fusion
  318.8 0.4 copy.48
  319.3 1.0 copy.49
  (129 shorter events, 3.6 us)
Async XLA Ops:
  6.5 286.2 %copy-start = (f32[1,512,512]{2,1,0:T(8,128)S(1)}, f32[1,512,512]{2,1,0:T(8,128)}, u32[]{:S(2)}) copy-start(f32[1,512,512]{2,1,0:T(8,128)} %param.15) | copy-start | bytes 3145732
  6.5 89.0 %all-reduce.3.cloned.1.call-start = ((), (), s32[]{:S(2)}) async-start(), calls=%async_computation.2 | async-start | bytes 3145728 | tf_op jit(solution)/shard_map/psum | solution.py:80
  6.6 12.2 %copy-start.17 = (f32[128]{0:T(128)}, f32[128]{0:T(128)S(1)}, u32[]{:S(2)}) copy-start(f32[128]{0:T(128)S(1)} %fusion.45) | copy-start | bytes 1540
  6.6 12.2 %copy-start.28 = (s32[4,8]{1,0:T(4,128)S(1)}, s32[4,8]{1,0:T(4,128)}, u32[]{:S(2)}) copy-start(s32[4,8]{1,0:T(4,128)} %param.12) | copy-start | bytes 388
  6.6 13.0 %copy-start.29 = (s32[8]{0:T(128)S(1)}, s32[8]{0:T(128)}, u32[]{:S(2)}) copy-start(s32[8]{0:T(128)} %param.11) | copy-start | bytes 100
  9.0 23.7 %copy-start.1 = (f32[256,3,4,64]{0,3,2,1:T(8,128)}, f32[256,3,4,64]{0,3,2,1:T(8,128)S(1)}, u32[]{:S(2)}) copy-start(f32[256,3,4,64]{0,3,2,1:T(8,128)S(1)} %fusion.12) | copy-start | bytes 2359300
  9.0 23.7 %collective-permute-start = (f32[3,1,4,64,256]{4,3,2,0,1:T(8,128)S(1)}, f32[3,1,4,64,256]{4,3,2,0,1:T(8,128)S(1)}, u32[]{:S(2)}, u32[]{:S(2)}) collective-permute-start(f32[3,1,4,64,256]{4,3,2,0,1:T(8,128)S(1)} %bitcast.258), channel_id=1, source_target_pairs={{0,32},{32,64},{64,96},{96,128},{128,160},{160,192},{192,224},{224... | collective-permute-start | bytes 2359304 | tf_op jit(solution)/shard_map/ppermute | solution.py:15
  11.5 22.1 %collective-permute-start.1 = (f32[3,1,4,64,256]{4,3,2,0,1:T(8,128)S(1)}, f32[3,1,4,64,256]{4,3,2,0,1:T(8,128)}, u32[]{:S(2)}, u32[]{:S(2)}) collective-permute-start(f32[3,1,4,64,256]{4,3,2,0,1:T(8,128)S(1)} %bitcast.259), channel_id=1, source_target_pairs={{32,0},{64,32},{96,64},{128,96},{160,128},{192,160},{224,192},{0,2... | collective-permute-start | bytes 2359304 | tf_op jit(solution)/shard_map/ppermute | solution.py:18
  15.6 19.9 %copy-start.18 = (s32[4]{0:T(128)}, s32[4]{0:T(128)S(1)}, u32[]{:S(2)}) copy-start(s32[4]{0:T(128)S(1)} %get-tuple-element.70) | copy-start | bytes 52
  18.8 230.9 %all-reduce.5.cloned.1.call-start = ((), (), s32[]{:S(2)}) async-start(), calls=%async_computation.3 | async-start | bytes 3145728 | tf_op jit(solution)/shard_map/psum | solution.py:91
  19.2 28.2 %copy-start.19 = (pred[4]{0:T(512)(128)(4,1)}, pred[4]{0:T(512)(128)(4,1)S(1)}, u32[]{:S(2)}) copy-start(pred[4]{0:T(512)(128)(4,1)S(1)} %compare_and_fusion.2) | copy-start | bytes 16
  19.3 29.6 %copy-start.20 = (pred[4]{0:T(512)(128)(4,1)}, pred[4]{0:T(512)(128)(4,1)S(1)}, u32[]{:S(2)}) copy-start(pred[4]{0:T(512)(128)(4,1)S(1)} %compare_and_fusion.4) | copy-start | bytes 16
  19.3 30.9 %copy-start.21 = (pred[4]{0:T(512)(128)(4,1)}, pred[4]{0:T(512)(128)(4,1)S(1)}, u32[]{:S(2)}) copy-start(pred[4]{0:T(512)(128)(4,1)S(1)} %compare_and_fusion.5) | copy-start | bytes 16
  19.3 31.1 %copy-start.22 = (pred[4]{0:T(512)(128)(4,1)}, pred[4]{0:T(512)(128)(4,1)S(1)}, u32[]{:S(2)}) copy-start(pred[4]{0:T(512)(128)(4,1)S(1)} %compare_and_fusion.6) | copy-start | bytes 16
  19.4 31.2 %copy-start.23 = (pred[4]{0:T(512)(128)(4,1)}, pred[4]{0:T(512)(128)(4,1)S(1)}, u32[]{:S(2)}) copy-start(pred[4]{0:T(512)(128)(4,1)S(1)} %compare_and_fusion.7) | copy-start | bytes 16
  19.4 31.4 %copy-start.24 = (pred[4]{0:T(512)(128)(4,1)}, pred[4]{0:T(512)(128)(4,1)S(1)}, u32[]{:S(2)}) copy-start(pred[4]{0:T(512)(128)(4,1)S(1)} %compare_and_fusion.8) | copy-start | bytes 16
  19.7 31.8 %copy-start.25 = (pred[4]{0:T(512)(128)(4,1)}, pred[4]{0:T(512)(128)(4,1)S(1)}, u32[]{:S(2)}) copy-start(pred[4]{0:T(512)(128)(4,1)S(1)} %compare_and_fusion.9) | copy-start | bytes 16
  19.8 32.1 %copy-start.26 = (pred[4]{0:T(512)(128)(4,1)}, pred[4]{0:T(512)(128)(4,1)S(1)}, u32[]{:S(2)}) copy-start(pred[4]{0:T(512)(128)(4,1)S(1)} %compare_and_fusion.3) | copy-start | bytes 16
  19.8 32.3 %copy-start.27 = (f32[4]{0:T(128)}, f32[4]{0:T(128)S(1)}, u32[]{:S(2)}) copy-start(f32[4]{0:T(128)S(1)} %broadcast_subtract_fusion) | copy-start | bytes 52
  32.7 0.9 copy-start.16
  47.5 2.8 copy-start.5
  47.5 3.0 copy-start.6
  48.9 1.7 copy-start.8
  50.3 1.2 copy-start.10
  50.4 1.2 copy-start.12
  50.6 1.4 copy-start.13
  52.1 1.6 copy-start.2
  55.3 3.9 %copy-start.33 = (s32[64]{0:T(128)S(1)}, s32[64]{0:T(128)}, u32[]{:S(2)}) copy-start(s32[64]{0:T(128)} %param.13) | copy-start | bytes 772
  55.4 5.0 %copy-start.32 = (s32[4]{0:T(128)S(1)}, s32[4]{0:T(128)}, u32[]{:S(2)}) copy-start(s32[4]{0:T(128)} %param.14) | copy-start | bytes 52
  59.3 0.5 copy-start.31
  112.2 142.2 %copy-start.3 = (f32[4,3,64,256]{3,2,1,0:T(8,128)S(1)}, f32[4,3,64,256]{3,2,1,0:T(8,128)}, u32[]{:S(2)}) copy-start(f32[4,3,64,256]{3,2,1,0:T(8,128)} %gather_fusion.7) | copy-start | bytes 2359300
  112.2 142.2 %copy-start.4 = (f32[4,3,64,256]{3,2,1,0:T(8,128)S(1)}, f32[4,3,64,256]{3,2,1,0:T(8,128)}, u32[]{:S(2)}) copy-start(f32[4,3,64,256]{3,2,1,0:T(8,128)} %gather_fusion.5) | copy-start | bytes 2359300
  249.7 4.7 %copy-start.7 = (f32[4,3,64,256]{3,2,1,0:T(8,128)S(1)}, f32[4,3,64,256]{3,2,1,0:T(8,128)}, u32[]{:S(2)}) copy-start(f32[4,3,64,256]{3,2,1,0:T(8,128)} %gather_fusion.3) | copy-start | bytes 2359300
  249.7 4.7 %copy-start.9 = (f32[4,3,64,256]{3,2,1,0:T(8,128)S(1)}, f32[4,3,64,256]{3,2,1,0:T(8,128)}, u32[]{:S(2)}) copy-start(f32[4,3,64,256]{3,2,1,0:T(8,128)} %gather_fusion.2) | copy-start | bytes 2359300
  249.7 4.7 %copy-start.11 = (f32[4,3,64,256]{3,2,1,0:T(8,128)S(1)}, f32[4,3,64,256]{3,2,1,0:T(8,128)}, u32[]{:S(2)}) copy-start(f32[4,3,64,256]{3,2,1,0:T(8,128)} %gather_fusion.1) | copy-start | bytes 2359300
  249.7 4.7 %copy-start.14 = (f32[3,1,4,64,128]{4,3,2,1,0:T(8,128)S(1)}, f32[3,1,4,64,128]{4,3,2,1,0:T(8,128)}, u32[]{:S(2)}) copy-start(f32[3,1,4,64,128]{4,3,2,1,0:T(8,128)} %param.10) | copy-start | bytes 1179652
  249.7 4.7 %copy-start.15 = (f32[4,64,256]{2,1,0:T(8,128)S(1)}, f32[4,64,256]{2,1,0:T(8,128)}, u32[]{:S(2)}) copy-start(f32[4,64,256]{2,1,0:T(8,128)} %get-tuple-element.40) | copy-start | bytes 786436
  262.1 1.1 copy-start.30
  296.2 20.6 %all-to-all-start.1 = ((f32[3,1,4,64,128]{4,2,0,1,3:T(4,128)}), f32[3,1,4,64,128]{4,2,0,1,3:T(4,128)S(1)}, u32[]{:S(2)}, u32[]{:S(2)}) async-start(f32[3,1,4,64,128]{4,2,0,1,3:T(4,128)} %reshape.459), calls=%async_computation.1 | async-start | bytes 786432 | tf_op jit(solution)/shard_map/all_to_all | solution.py:113
Sparse Core Ops, SparseCore 0:
  18.9 76.5 all-reduce.2
  98.9 150.7 all-reduce.4
where the time goes:
time: 328 us; the launch traced here: 327 us
  waiting for transfers between devices  196 us (60%)
  local copies, waits for them, and re-layouts  50.8 us (15%)
  blocking collectives  27.5 us (8%)
  matrix products  17.6 us (5%)
  between operations  14.4 us (4%)
  starting transfers between devices  12.1 us (4%)
  other arithmetic  8.77 us (3%)
    psum x1, waiting for transfers between devices, local(): summed = lax.psum(stress, ('kx', 'real'))  134 us
    psum x1, waiting for transfers between devices, local(): low_fields = lax.psum(own_low, 'kx')  35.1 us
    all_to_all x1, blocking collectives, local(): lax.all_to_all(flat_out, ('kx', 'ht'), split_axis=3, concat_axis=3, tiled...  27.5 us
    all_to_all x1, waiting for transfers between devices, local(): lax.all_to_all(applied, ('kx', 'ht'), split_axis=3, concat_axis=3, tiled=...  14.2 us
    ppermute x1, waiting for transfers between devices, extended_2(): lax.ppermute(lax.slice_in_dim(block, block.shape[dim] - width, None, axis...  12.9 us
    gather x8, local copies, waits for them, and re-layouts, local(): partner = jnp.take(extended, local_partner[:, member], axis=2)  12 us
    unnamed x84, local copies, waits for them, and re-layouts  11.8 us
    slice x1, local copies, waits for them, and re-layouts, local(): low_one = low_fields[:, :, member:member + 1]  7.67 us
  transfers between devices with their start and end apart: 5, of which 4 were waited for; matrix products, arithmetic and copies ran while one was open for 15% of the time, Pallas kernels for 0%

commit v1 on v0

--- a/solution.py
+++ b/solution.py
@@ -88,7 +88,7 @@
         stresses.append(jnp.sum(weighted, axis=(1, 2)))
     stress = jnp.stack(stresses, axis=1)
     nonlinear = jnp.dot(high_low, backward, precision=highest)
-    summed = lax.psum(stress, ("kx", "real"))
+    summed = lax.psum(lax.psum(stress, "real"), "kx")
     low_forcing = jnp.dot(summed / realizations, backward, precision=highest)
     forcing = nonlinear * high_mask[None, None, :, None, None]
     forcing = (

time: 328 us -> 300 us (0.915)
  waiting for transfers between devices: 196 us -> 177 us
  other arithmetic: 8.77 us -> 20.8 us
  local copies, waits for them, and re-layouts: 50.8 us -> 40.8 us
  matrix products: 17.6 us -> 11.3 us
  blocking collectives: 27.5 us -> 23.4 us
    psum x1, waiting for transfers between devices: 134 us -> 53.4 us  [local(): summed = lax.psum(lax.psum(stress, 'real'), 'kx')]
    psum x1, waiting for transfers between devices: 35.1 us -> 93.7 us  [local(): low_fields = lax.psum(own_low, 'kx')]
    unnamed x84 -> x78, local copies, waits for them, and re-layouts: 11.8 us -> 1.48 us
    select_n x16, other arithmetic: 3.58 us -> 9.24 us  [local(): partner = jnp.take(extended, local_partner[:, member], axis=2)]
    mul x1 -> x8, other arithmetic: 1.39 us -> 5.86 us  [local(): high_low = high_low + low_one * partner[1:2] + partner * low_one[1:2]]
    all_to_all x1, blocking collectives: 27.5 us -> 23.4 us  [local(): lax.all_to_all(flat_out, ('kx', 'ht'), split_axis=3, concat_axis=3, tiled...]
    dot_general x1, matrix products: 5.87 us -> 2.44 us  [local(): nonlinear = jnp.dot(high_low, backward, precision=highest)]
  transfers between devices with their start and end apart: 5 -> 5, of which waited for: 4 -> 4; matrix products, arithmetic and copies ran while one was open for 15% -> 2% of each run, Pallas kernels for 0% -> 0%
where the time goes in v1:
time: 300 us; the launch traced here: 299 us
  waiting for transfers between devices  177 us (59%)
  local copies, waits for them, and re-layouts  40.8 us (14%)
  blocking collectives  23.4 us (8%)
  other arithmetic  20.8 us (7%)
  between operations  14.4 us (5%)
  starting transfers between devices  12.2 us (4%)
  matrix products  11.3 us (4%)
    psum x1, waiting for transfers between devices, local(): low_fields = lax.psum(own_low, 'kx')  93.7 us
    psum x1, waiting for transfers between devices, local(): summed = lax.psum(lax.psum(stress, 'real'), 'kx')  53.4 us
    all_to_all x1, blocking collectives, local(): lax.all_to_all(flat_out, ('kx', 'ht'), split_axis=3, concat_axis=3, tiled...  23.4 us
    ppermute x1, waiting for transfers between devices, extended_2(): lax.ppermute(lax.slice_in_dim(block, block.shape[dim] - width, None, axis...  14.9 us
    all_to_all x1, waiting for transfers between devices, local(): lax.all_to_all(applied, ('kx', 'ht'), split_axis=3, concat_axis=3, tiled=...  14.3 us
    gather x8, local copies, waits for them, and re-layouts, local(): partner = jnp.take(extended, local_partner[:, member], axis=2)  12 us
    select_n x16, other arithmetic, local(): partner = jnp.take(extended, local_partner[:, member], axis=2)  9.24 us
    slice x1, local copies, waits for them, and re-layouts, local(): low_one = low_fields[:, :, member:member + 1]  7.66 us
  transfers between devices with their start and end apart: 5, of which 4 were waited for; matrix products, arithmetic and copies ran while one was open for 2% of the time, Pallas kernels for 0%

profile of v1, /device:TPU:1, one launch (start us, length us, event | category | flops | bytes accessed | tf_op | source)
XLA Modules:
  0.0 299.5 jit_solution(11660636074015779274)
XLA Ops:
  6.6 2.4 fusion.12
  9.0 2.5 collective-permute-start
  11.5 4.0 %collective-permute-start.1 = (f32[3,1,4,64,256]{4,3,2,0,1:T(8,128)S(1)}, f32[3,1,4,64,256]{4,3,2,0,1:T(8,128)}, u32[]{:S(2)}, u32[]{:S(2)}) collective-permute-start(f32[3,1,4,64,256]{4,3,2,0,1:T(8,128)S(1)} %bitcast.259), channel_id=1, source_target_pairs={{32,0},{64,32},{96,64},{128,96},{160,128},{192,160},{224,192},{0,2... | collective-permute-start | bytes 2359304 | tf_op jit(solution)/shard_map/ppermute | solution.py:18
  15.6 0.8 fusion.41
  16.3 0.3 slice_reduce_fusion.7
  16.9 0.8 fusion.38
  17.8 14.9 %collective-permute-done = f32[3,1,4,64,256]{4,3,2,0,1:T(8,128)S(1)} collective-permute-done((f32[3,1,4,64,256]{4,3,2,0,1:T(8,128)S(1)}, f32[3,1,4,64,256]{4,3,2,0,1:T(8,128)S(1)}, u32[]{:S(2)}, u32[]{:S(2)}) %collective-permute-start) | collective-permute-done | bytes 786464 | tf_op jit(solution)/shard_map/ppermute | solution.py:15
  32.7 0.9 copy-done.27
  33.6 1.8 maximum_bitcast_fusion
  35.4 1.5 gather_fusion
  36.9 1.5 gather_fusion.1
  38.3 1.3 bitcast_select_fusion.9
  39.7 0.8 slice_bitcast_fusion.7
  40.7 0.8 slice_bitcast_fusion.6
  41.5 1.5 gather_fusion.2
  43.0 1.3 bitcast_select_fusion.7
  44.3 0.8 slice_bitcast_fusion.5
  45.1 1.6 gather_fusion.3
  46.7 1.3 bitcast_select_fusion.6
  48.0 0.8 slice_bitcast_fusion.4
  48.8 1.5 gather_fusion.4
  50.3 1.3 bitcast_select_fusion.5
  51.5 0.8 slice_bitcast_fusion.3
  52.4 1.5 gather_fusion.5
  53.9 1.3 bitcast_select_fusion.4
  55.1 0.8 slice_bitcast_fusion.2
  56.0 1.5 gather_fusion.6
  57.5 1.3 bitcast_select_fusion.3
  58.7 0.8 slice_bitcast_fusion.1
  59.6 1.5 gather_fusion.7
  61.1 1.4 bitcast_select_fusion.2
  62.9 1.6 multiply_reduce_fusion
  65.5 0.8 stack.34
  66.3 4.8 %stack.35 = f32[3,8,64,256]{3,1,2,0:T(8,128)} concatenate(f32[3,1,64,256]{3,1,2,0:T(1,128)S(1)} %stack.27, f32[3,1,64,256]{3,1,2,0:T(1,128)S(1)} %stack.28, f32[3,1,64,256]{3,1,2,0:T(1,128)S(1)} %stack.29, f32[3,1,64,256]{3,1,2,0:T(1,128)S(1)} %stack.30, f32[3,1,64,256]{3,1,2,0:T(1,128)S(1)} %stack.31, f32[3,1,64,256]{3,1,2,0:T(1,128)S(1)} %stack.32, ...), dimensions={1} | concatenate | bytes 3145728 | tf_op jit(solution)/shard_map/stack | solution.py:89
  71.2 0.2 all-reduce.6.cloned.1.call-start
  71.5 2.5 convolution_bitcast_fusion
  73.9 53.4 %all-reduce.4.cloned.1.call-done = f32[3,8,64,256]{3,1,2,0:T(8,128)} async-done(((f32[3,8,64,256]{3,1,2,0:T(8,128)}), f32[3,8,64,256]{3,1,2,0:T(8,128)}) %all-reduce.4.cloned.1.call-update) | async-done | bytes 1572880 | tf_op jit(solution)/shard_map/psum | solution.py:91
  127.6 93.7 %all-reduce.6.cloned.1.call-done = (f32[3,1,8,64,256]{4,2,3,0,1:T(8,128)}, f32[3,8,64,256]{3,1,2,0:T(8,128)}) async-done(((f32[3,1,8,64,256]{4,2,3,0,1:T(8,128)}, f32[3,8,64,256]{3,1,2,0:T(8,128)}), (f32[3,1,8,64,256]{4,2,3,0,1:T(8,128)}, f32[3,8,64,256]{3,1,2,0:T(8,128)})) %all-reduce.6.cloned.1.call-update) | async-done | bytes 3145744 | tf_op jit(solution)/shard_map/psum | solution.py:80
  221.3 7.7 %fusion.51 = (f32[3,1,1,64,256]{4,2,3,0,1:T(1,128)S(1)}, f32[3,1,1,64,256]{4,2,3,0,1:T(1,128)S(1)}, f32[3,1,1,64,256]{4,2,3,0,1:T(1,128)S(1)}, f32[3,1,1,64,256]...) fusion(f32[3,1,8,64,256]{4,2,3,0,1:T(8,128)} %get-tuple-element.23), kind=kLoop, calls=%fused_computation.172 | loop fusion | bytes 3145728 | tf_op jit(solution)/shard_map/slice | solution.py:85
  229.0 3.3 %fusion.52 = (f32[1,1,1,64,256]{4,2,3,0,1:T(1,128)S(1)}, f32[1,1,1,64,256]{4,2,3,0,1:T(1,128)S(1)}, f32[1,1,1,64,256]{4,2,3,0,1:T(1,128)S(1)}, f32[1,1,1,64,256]...) fusion(f32[3,1,8,64,256]{4,2,3,0,1:T(8,128)} %get-tuple-element.23), kind=kLoop, calls=%fused_computation.173 | loop fusion | bytes 1048576 | tf_op jit(solution)/shard_map/slice | solution.py:86
  232.6 1.9 fusion
  234.5 0.5 fusion.50
  235.4 2.4 fusion.6
  237.8 0.3 copy.38
  238.1 0.5 copy.101
  238.6 1.0 gather_fusion.8
  239.7 0.2 fusion.7
  239.9 0.4 copy.55
  240.3 0.6 reshape.457
  240.9 23.4 %all_to_all.10 = f32[3,1,4,64,128]{4,2,0,1,3:T(4,128)S(1)} all-to-all(f32[3,1,4,64,128]{4,2,0,1,3:T(4,128)S(1)} %reshape.457), channel_id=1, replica_groups=mesh['kx'=8,'ht'=8,'real'=4] {'kx','ht'}, dimensions={3} | all-to-all | bytes 786432 | tf_op jit(solution)/shard_map/all_to_all | solution.py:106
  264.4 0.5 reshape.287
  264.9 0.2 reshape.455
  265.2 1.5 convolution_bitcast_fusion.1
  266.6 0.6 copy.56
  267.3 1.3 reshape.459
  268.6 5.5 %all-to-all-start.1 = ((f32[3,1,4,64,128]{4,2,0,1,3:T(4,128)}), f32[3,1,4,64,128]{4,2,0,1,3:T(4,128)S(1)}, u32[]{:S(2)}, u32[]{:S(2)}) async-start(f32[3,1,4,64,128]{4,2,0,1,3:T(4,128)} %reshape.459), calls=%async_computation.1 | async-start | bytes 786432 | tf_op jit(solution)/shard_map/all_to_all | solution.py:113
  274.0 0.8 scatter_custom_fusion
  274.9 14.3 %all-to-all-done.1 = f32[3,1,4,64,128]{4,2,0,1,3:T(4,128)S(1)} async-done(((f32[3,1,4,64,128]{4,2,0,1,3:T(4,128)}), f32[3,1,4,64,128]{4,2,0,1,3:T(4,128)S(1)}, u32[]{:S(2)}, u32[]{:S(2)}) %all-to-all-start.1) | async-done | bytes 393248 | tf_op jit(solution)/shard_map/all_to_all | solution.py:113
  289.2 0.5 reshape.460
  289.7 0.2 copy.100
  289.9 1.1 gather_fusion.9
  291.0 0.2 bitcast_select_fusion
  291.2 0.4 copy.48
  291.6 1.0 copy.49
  (130 shorter events, 2.2 us)
Async XLA Ops:
  6.5 258.6 %copy-start = (f32[1,512,512]{2,1,0:T(8,128)S(1)}, f32[1,512,512]{2,1,0:T(8,128)}, u32[]{:S(2)}) copy-start(f32[1,512,512]{2,1,0:T(8,128)} %param.15) | copy-start | bytes 3145732
  6.5 120.9 %all-reduce.4.cloned.1.call-start = ((), (), s32[]{:S(2)}) async-start(), calls=%async_computation.2 | async-start | bytes 3145728 | tf_op jit(solution)/shard_map/psum | solution.py:91
  9.0 23.7 %copy-start.1 = (f32[256,3,4,64]{0,3,2,1:T(8,128)}, f32[256,3,4,64]{0,3,2,1:T(8,128)S(1)}, u32[]{:S(2)}) copy-start(f32[256,3,4,64]{0,3,2,1:T(8,128)S(1)} %fusion.12) | copy-start | bytes 2359300
  9.0 23.7 %collective-permute-start = (f32[3,1,4,64,256]{4,3,2,0,1:T(8,128)S(1)}, f32[3,1,4,64,256]{4,3,2,0,1:T(8,128)S(1)}, u32[]{:S(2)}, u32[]{:S(2)}) collective-permute-start(f32[3,1,4,64,256]{4,3,2,0,1:T(8,128)S(1)} %bitcast.258), channel_id=1, source_target_pairs={{0,32},{32,64},{64,96},{96,128},{128,160},{160,192},{192,224},{224... | collective-permute-start | bytes 2359304 | tf_op jit(solution)/shard_map/ppermute | solution.py:15
  11.5 22.1 %collective-permute-start.1 = (f32[3,1,4,64,256]{4,3,2,0,1:T(8,128)S(1)}, f32[3,1,4,64,256]{4,3,2,0,1:T(8,128)}, u32[]{:S(2)}, u32[]{:S(2)}) collective-permute-start(f32[3,1,4,64,256]{4,3,2,0,1:T(8,128)S(1)} %bitcast.259), channel_id=1, source_target_pairs={{32,0},{64,32},{96,64},{128,96},{160,128},{192,160},{224,192},{0,2... | collective-permute-start | bytes 2359304 | tf_op jit(solution)/shard_map/ppermute | solution.py:18
  32.7 0.9 copy-start.27
  38.3 2.2 copy-start.4
  61.0 1.6 copy-start.2
  61.0 1.6 copy-start.21
  61.0 1.6 copy-start.22
  61.0 1.6 copy-start.23
  61.1 1.6 copy-start.24
  61.1 1.7 copy-start.25
  61.1 1.8 copy-start.26
  66.3 5.1 %copy-start.28 = (s32[8]{0:T(128)S(1)}, s32[8]{0:T(128)}, u32[]{:S(2)}) copy-start(s32[8]{0:T(128)} %param.11) | copy-start | bytes 100
  71.2 150.1 %all-reduce.6.cloned.1.call-start = ((), (), s32[]{:S(2)}) async-start(), calls=%async_computation.3 | async-start | bytes 6291456 | tf_op jit(solution)/shard_map/psum | solution.py:80
  71.4 56.0 %copy-start.30 = (s32[64]{0:T(128)S(1)}, s32[64]{0:T(128)}, u32[]{:S(2)}) copy-start(s32[64]{0:T(128)} %param.13) | copy-start | bytes 772
  71.4 56.0 %copy-start.29 = (s32[4]{0:T(128)S(1)}, s32[4]{0:T(128)}, u32[]{:S(2)}) copy-start(s32[4]{0:T(128)} %param.14) | copy-start | bytes 52
  221.3 13.8 %copy-start.16 = (f32[4,64,256]{2,1,0:T(8,128)S(1)}, f32[4,64,256]{2,1,0:T(8,128)}, u32[]{:S(2)}) copy-start(f32[4,64,256]{2,1,0:T(8,128)} %get-tuple-element.45) | copy-start | bytes 786436
  221.3 13.9 %copy-start.17 = (f32[4,64,256]{2,1,0:T(8,128)S(1)}, f32[4,64,256]{2,1,0:T(8,128)}, u32[]{:S(2)}) copy-start(f32[4,64,256]{2,1,0:T(8,128)} %get-tuple-element.47) | copy-start | bytes 786436
  221.3 13.9 %copy-start.18 = (f32[4,64,256]{2,1,0:T(8,128)S(1)}, f32[4,64,256]{2,1,0:T(8,128)}, u32[]{:S(2)}) copy-start(f32[4,64,256]{2,1,0:T(8,128)} %get-tuple-element.49) | copy-start | bytes 786436
  221.3 13.9 %copy-start.19 = (f32[4,64,256]{2,1,0:T(8,128)S(1)}, f32[4,64,256]{2,1,0:T(8,128)}, u32[]{:S(2)}) copy-start(f32[4,64,256]{2,1,0:T(8,128)} %get-tuple-element.51) | copy-start | bytes 786436
  221.3 13.9 %copy-start.20 = (f32[4,64,256]{2,1,0:T(8,128)S(1)}, f32[4,64,256]{2,1,0:T(8,128)}, u32[]{:S(2)}) copy-start(f32[4,64,256]{2,1,0:T(8,128)} %get-tuple-element.53) | copy-start | bytes 786436
  229.0 3.6 %copy-start.13 = (f32[3,8,64,256]{3,1,2,0:T(8,128)S(1)}, f32[3,8,64,256]{3,1,2,0:T(8,128)}, u32[]{:S(2)}) copy-start(f32[3,8,64,256]{3,1,2,0:T(8,128)} %get-tuple-element.24) | copy-start | bytes 4718596
  232.3 2.9 copy-start.15
  232.3 2.9 copy-start.12
  232.4 2.8 copy-start.11
  232.4 2.8 copy-start.10
  232.5 2.8 copy-start.9
  232.5 2.7 copy-start.3
  232.5 2.7 copy-start.5
  232.5 2.7 copy-start.6
  232.5 2.7 copy-start.7
  232.6 2.8 copy-start.8
  232.6 2.8 copy-start.14
  268.6 20.6 %all-to-all-start.1 = ((f32[3,1,4,64,128]{4,2,0,1,3:T(4,128)}), f32[3,1,4,64,128]{4,2,0,1,3:T(4,128)S(1)}, u32[]{:S(2)}, u32[]{:S(2)}) async-start(f32[3,1,4,64,128]{4,2,0,1,3:T(4,128)} %reshape.459), calls=%async_computation.1 | async-start | bytes 786432 | tf_op jit(solution)/shard_map/all_to_all | solution.py:113
Sparse Core Ops, SparseCore 0:
  71.3 56.0 all-reduce.3
  129.8 91.4 all-reduce.5
